TPU v7x, 32 devices: a whole 2x2x4 slice. The times are simulated.
32 devices in a mesh: groups: 2 (over y), tm: 4 (over z), dp: 2 (over x), head: 2 (over core).
Axes of the slice: x: 2, y: 2, z: 4, core: 2. Of those that a mesh axis runs over, the one named last changes fastest.
Arguments:
- frames: bfloat16 [4, 7168, 512], P(('groups', 'dp'), 'tm', 'head'), parts along dimension 0, may hold values from -8 to 8
- lengths: int32 [4], P(('groups', 'dp')), parts along dimension 0, may hold values from 1792 to 7168, as said below
- down_weights: float32 [4, 512], P(None, 'head'), may hold values from 0.1 to 0.4
- w_query: bfloat16 [512, 256], P(None, 'head'), may hold values from -0.79549513 to 0.79549513
- w_key: bfloat16 [512, 256], P(None, 'head'), may hold values from -0.79549513 to 0.79549513
- w_value: bfloat16 [512, 96], P(None, 'head'), may hold values from -0.25 to 0.25
- w_out: bfloat16 [96, 512], P('head'), may hold values from -0.625 to 0.625
- conv_in: bfloat16 [512, 2, 512], P(None, None, 'head'), may hold values from -0.25 to 0.25
- conv_taps: float32 [31, 512], P(None, 'head'), may hold values from -1.8 to 1.8
- conv_out: bfloat16 [512, 512], P('head'), may hold values from -0.25 to 0.25
- bypass: float32 [512], P('head'), may hold values from 0.2 to 0.9
Outputs:
- stack_out: bfloat16 [4, 7168, 512], P(('groups', 'dp'), 'tm', 'head'), parts along dimension 0
There are 2 independent parts, one for each index of `groups`. A program takes and returns all parts, laid end to end along the dimension named above; an argument that names none is the same for every part. Nothing has to cross between parts.
Inputs may be any that keep to these rules, and one draw needn't show every extreme that they name: `lengths`: valid frames of each recording; the later slots are padding. In every part some recording has all 7168 frames.
All inputs are finite; a program needn't handle non-finite values.
Results may differ from a plain program's by a relative error of at most 0.009.
Values may be sent and summed in bfloat16 or wider, within the bound.
No kernel may reach another device: no remote copies, remote signals or barrier semaphores. Data moves between devices by JAX's collectives and lax.ppermute only.
A program may use at most 64 MiB of HBM per device.

v0:
```python
import jax
import jax.numpy as jnp
from jax import lax
from jax.sharding import PartitionSpec as P

QDIM = 32
VDIM = 12


def with_halo(block, sides, width):
    for axis, dim in sides:
        count = lax.axis_size(axis)
        forward = [(i, i + 1) for i in range(count - 1)]
        backward = [(target, source) for source, target in forward]
        low = lax.ppermute(
            lax.slice_in_dim(block, block.shape[dim] - width, None, axis=dim), axis, forward
        )
        high = lax.ppermute(lax.slice_in_dim(block, 0, width, axis=dim), axis, backward)
        block = jnp.concatenate([low, block, high], axis=dim)
    return block


def shards(
    frames,
    lengths,
    down_weights,
    w_query,
    w_key,
    w_value,
    w_out,
    conv_in,
    conv_taps,
    conv_out,
    bypass,
):
    records, frame_count, channels = frames.shape
    quarter = frame_count // 4
    group_size = lax.axis_size("tm")
    group_index = lax.axis_index("tm")
    positions = group_index * frame_count + jnp.arange(frame_count)
    frame_live = positions[None, :] < lengths[:, None]
    masked = jnp.where(frame_live[:, :, None], frames, jnp.zeros_like(frames))
    grouped = masked.reshape(records, quarter, 4, channels).astype(jnp.float32)
    reduced = jnp.sum(grouped * down_weights[None, None], axis=2).astype(jnp.bfloat16)
    live_rows = (lengths + 3) // 4
    row_index = group_index * quarter + jnp.arange(quarter)
    row_live = row_index[None, :] < live_rows[:, None]
    full_rows = lax.all_gather(reduced, "head", axis=2, tiled=True)
    heads_here = w_query.shape[1] // QDIM
    queries = jnp.einsum("rsd,dk->rsk", full_rows, w_query, preferred_element_type=jnp.float32)
    queries = queries.astype(jnp.bfloat16).reshape(records, quarter, heads_here, QDIM)
    segment = lax.all_gather(full_rows, "tm", axis=1, tiled=True)
    keys_t = jnp.einsum("rnd,dk->rkn", segment, w_key, preferred_element_type=jnp.float32)
    values_t = jnp.einsum("rnd,dk->rkn", segment, w_value, preferred_element_type=jnp.float32)
    packed = jnp.concatenate([keys_t, values_t], axis=1).astype(jnp.bfloat16)
    key_width = heads_here * QDIM
    key_block = 2 * quarter
    block_count = group_size // 2
    score_scale = QDIM ** (-0.5)
    key_offsets = jnp.arange(key_block)
    initial = (
        jnp.full((records, heads_here, quarter), -1e30, jnp.float32),
        jnp.zeros((records, heads_here, quarter), jnp.float32),
        jnp.zeros((records, heads_here, quarter, VDIM), jnp.float32),
    )

    def merge_block(query_set, segment, key_live, running):
        top_score, denominator, weighted = running
        count_rows = segment.shape[0]
        key_rows = segment[:, :key_width].reshape(count_rows, heads_here, QDIM, key_block)
        value_rows = segment[:, key_width:].reshape(count_rows, heads_here, VDIM, key_block)
        scores = (
            jnp.einsum("rqhd,rhdk->rhqk", query_set, key_rows, preferred_element_type=jnp.float32)
            * score_scale
        )
        scores = jnp.where(key_live[:, None, None, :], scores, jnp.float32(-1e30))
        new_top = jnp.maximum(top_score, jnp.max(scores, axis=-1))
        factor = jnp.exp(top_score - new_top)
        expo = jnp.where(
            key_live[:, None, None, :], jnp.exp(scores - new_top[..., None]), jnp.float32(0.0)
        )
        denominator = denominator * factor + jnp.sum(expo, axis=-1)
        weighted = weighted * factor[..., None] + jnp.einsum(
            "rhqk,rhvk->rhqv",
            expo.astype(jnp.bfloat16),
            value_rows,
            preferred_element_type=jnp.float32,
        )
        return (new_top, denominator, weighted)

    def advance_all(block_index, running):
        first_key = block_index * key_block
        segment = lax.dynamic_slice_in_dim(packed, first_key, key_block, 2)
        key_live = (first_key + key_offsets)[None, :] < live_rows[:, None]
        return merge_block(queries, segment, key_live, running)

    top_score, denominator, weighted = lax.fori_loop(0, block_count, advance_all, initial)
    attended = weighted / denominator[..., None]
    attended = (
        jnp.transpose(attended, (0, 2, 1, 3))
        .reshape(records, quarter, heads_here * VDIM)
        .astype(jnp.bfloat16)
    )
    partial_value = jnp.einsum("rsv,vd->rsd", attended, w_out, preferred_element_type=jnp.float32)
    attn_half = lax.psum_scatter(
        partial_value.astype(jnp.bfloat16), "head", scatter_dimension=2, tiled=True
    ).astype(jnp.float32)
    after_attn = (reduced.astype(jnp.float32) + attn_half).astype(jnp.bfloat16)
    attn_rows = lax.all_gather(after_attn, "head", axis=2, tiled=True)
    gates = jnp.einsum("rsd,dgc->rsgc", attn_rows, conv_in, preferred_element_type=jnp.float32)
    gated = gates[:, :, 0] * jax.nn.sigmoid(gates[:, :, 1])
    gated = jnp.where(row_live[:, :, None], gated, jnp.float32(0.0)).astype(jnp.bfloat16)
    reach = conv_taps.shape[0] // 2
    padded = with_halo(gated, (("tm", 1),), reach)
    depthwise = jnp.zeros((records, quarter, channels), jnp.float32)
    for tap_index in range(conv_taps.shape[0]):
        depthwise = depthwise + conv_taps[tap_index][None, None, :] * padded[
            :, tap_index : tap_index + quarter
        ].astype(jnp.float32)
    hidden = jax.nn.silu(depthwise).astype(jnp.bfloat16)
    conv_part = jnp.einsum("rsc,cd->rsd", hidden, conv_out, preferred_element_type=jnp.float32)
    conv_half = lax.psum_scatter(
        conv_part.astype(jnp.bfloat16), "head", scatter_dimension=2, tiled=True
    ).astype(jnp.float32)
    stacked = after_attn.astype(jnp.float32) + conv_half
    upsampled = jnp.repeat(stacked, 4, axis=1)
    backdrop = frames.astype(jnp.float32)
    result = backdrop + bypass[None, None, :] * (upsampled - backdrop)
    return jnp.where(frame_live[:, :, None], result, jnp.float32(0.0)).astype(jnp.bfloat16)


def solution(mesh):
    in_specs = (
        P(("groups", "dp"), "tm", "head"),
        P(("groups", "dp")),
        P(None, "head"),
        P(None, "head"),
        P(None, "head"),
        P(None, "head"),
        P("head", None),
        P(None, None, "head"),
        P(None, "head"),
        P("head", None),
        P("head"),
    )
    out_specs = P(("groups", "dp"), "tm", "head")
    return jax.shard_map(shards, mesh=mesh, in_specs=in_specs, out_specs=out_specs, check_vma=False)
```

profile of v0, /device:TPU:0, one launch (start us, length us, event | category | flops | bytes accessed | tf_op | source)
XLA Modules:
  0.0 135.5 jit_solution(3686259870509432775)
XLA Ops:
  7.9 2.7 %select_convert_fusion = f32[1,1792,256]{2,1,0:T(8,128)} fusion(bf16[1,1792,256]{2,1,0:T(8,128)(2,1)} %param.13, pred[1792]{0:T(1024)(128)(4,1)S(1)} %add_compare_fusion), kind=kLoop, calls=%fused_computation.72 | loop fusion | flops 917504 | bytes 2754304 | tf_op jit(solution)/shard_map/convert_element_type | solution.py:43
  10.6 1.8 %reshape.448 = f32[1,448,4,256]{3,2,1,0:T(4,128)S(1)} reshape(f32[1,1792,256]{2,1,0:T(8,128)} %select_convert_fusion) | data formatting | bytes 3670016 | tf_op jit(solution)/shard_map/convert_element_type | solution.py:43
  12.5 1.3 multiply_reduce_fusion
  14.5 2.4 %all-gather = bf16[448,512]{1,0:T(8,128)(2,1)} all-gather(bf16[448,256]{1,0:T(8,128)(2,1)S(1)} %multiply_reduce_fusion), channel_id=2, replica_groups=mesh['groups'=2,'tm'=4,'dp'=2,'head'=2] {'head'}, dimensions={1}, use_global_device_ids=true | all-gather | bytes 688128 | tf_op jit(solution)/shard_map/all_gather | solution.py:48
  17.0 1.3 convolution_convert_fusion.4
  19.1 41.9 %all-gather.4.cloned.1.call-done = bf16[1792,512]{1,0:T(8,128)(2,1)} async-done(((bf16[448,512]{1,0:T(8,128)(2,1)}), bf16[1792,512]{1,0:T(8,128)(2,1)}) %all-gather.4.cloned.1.call-update) | async-done | bytes 1835024 | tf_op jit(solution)/shard_map/all_gather | solution.py:52
  61.0 2.4 %fusion.23 = bf16[1,128,1792]{2,1,0:T(8,128)(2,1)S(1)} fusion(bf16[1792,512]{1,0:T(8,128)(2,1)} %all-gather.4.cloned.1.call-done, bf16[512,128]{1,0:T(8,128)(2,1)S(1)} %copy-done.4), kind=kOutput, calls=%fused_computation.29 | convolution fusion | flops 235110400 | bytes 2424832 | tf_op jit(solution)/shard_map/rnd,dk->rkn/dot_general | solution.py:53
  64.1 25.0 %while.18 = (s32[]{:T(128)}, f32[1,4,448]{2,1,0:T(4,128)S(1)}, f32[1,4,448]{2,1,0:T(4,128)S(1)}, f32[1,4,448,12]{2,3,1,0:T(8,128)}, s32[1]{0:T(128)}, /*index=5*...) while((s32[]{:T(128)}, f32[1,4,448]{2,1,0:T(4,128)S(1)}, ...), condition=%wide.region_4.5_spmd.clone, body=%wide.region_1.4_spmd.clone.sunk | while | flops 162245888 | bytes 40058620 | solution.py:97
  64.1 4.8 %bitcast_reduce_fusion.2 = (f32[4,448]{1,0:T(4,128)S(1)}, f32[4,896,448]{1,2,0:T(8,128)}) fusion(pred[896]{0:T(1024)(128)(4,1)S(1)} %fusion.96, bf16[4,32,896]{2,1,0:T(8,128)(2,1)S(1)} %bitcast.144, bf16[1,448,4,32]{1,3,2,0:T(8,128)(2,1)} %get-tuple-element.312), kind=kOutput, calls=%fused_computation.2.clone.1 | convolution fusion | flops 107575552 | bytes 6774656 | tf_op jit(solution)/shard_map/while/body/eval_jaxpr/rqhd,rhdk->rhqk/dot_general | solution.py:73
  69.7 5.0 %fusion.99 = f32[1,4,448,12]{2,3,1,0:T(8,128)} fusion(bf16[4,12,896]{2,1,0:T(8,128)(2,1)} %reshape.460, f32[4,896,448]{1,2,0:T(8,128)} %get-tuple-element.280, f32[4,448]{1,0:T(4,128)S(1)} %bitcast.145, pred[896]{0:T(1024)(128)(4,1)S(1)} %fusion.96, f32[1,4,448,12]{2,3,1,0:T(8,128)} %get-tuple-element.297, f32[4,448]{1,0:T(4,128)S(1)} %get-tuple-element.281, ...), kind=kOutput, calls=%fused_computation.12.clone.1 | convolution fusion | flops 46627840 | bytes 6695809 | tf_op jit(solution)/shard_map/while/body/eval_jaxpr/rhqk,rhvk->rhqv/dot_general | solution.py:83
  74.7 1.8 %fusion.98 = f32[4,448]{1,0:T(4,128)S(1)} fusion(f32[4,896,448]{1,2,0:T(8,128)S(1)} %bitcast.143, f32[4,448]{1,0:T(4,128)S(1)} %bitcast.146, pred[896]{0:T(1024)(128)(4,1)S(1)} %fusion.96), kind=kLoop, calls=%fused_computation.7.clone.1 | loop fusion | flops 8026368 | bytes 6437760 | tf_op jit(solution)/shard_map/while/body/eval_jaxpr/reduce_sum | solution.py:82
  76.6 4.8 %bitcast_reduce_fusion.2 = (f32[4,448]{1,0:T(4,128)S(1)}, f32[4,896,448]{1,2,0:T(8,128)}) fusion(pred[896]{0:T(1024)(128)(4,1)S(1)} %fusion.96, bf16[4,32,896]{2,1,0:T(8,128)(2,1)S(1)} %bitcast.144, bf16[1,448,4,32]{1,3,2,0:T(8,128)(2,1)} %get-tuple-element.312), kind=kOutput, calls=%fused_computation.2.clone.1 | convolution fusion | flops 107575552 | bytes 6774656 | tf_op jit(solution)/shard_map/while/body/eval_jaxpr/rqhd,rhdk->rhqk/dot_general | solution.py:73
  82.1 5.0 %fusion.99 = f32[1,4,448,12]{2,3,1,0:T(8,128)} fusion(bf16[4,12,896]{2,1,0:T(8,128)(2,1)} %reshape.460, f32[4,896,448]{1,2,0:T(8,128)} %get-tuple-element.280, f32[4,448]{1,0:T(4,128)S(1)} %bitcast.145, pred[896]{0:T(1024)(128)(4,1)S(1)} %fusion.96, f32[1,4,448,12]{2,3,1,0:T(8,128)} %get-tuple-element.297, f32[4,448]{1,0:T(4,128)S(1)} %get-tuple-element.281, ...), kind=kOutput, calls=%fused_computation.12.clone.1 | convolution fusion | flops 46627840 | bytes 6695809 | tf_op jit(solution)/shard_map/while/body/eval_jaxpr/rhqk,rhvk->rhqv/dot_general | solution.py:83
  87.2 1.8 %fusion.98 = f32[4,448]{1,0:T(4,128)S(1)} fusion(f32[4,896,448]{1,2,0:T(8,128)S(1)} %bitcast.143, f32[4,448]{1,0:T(4,128)S(1)} %bitcast.146, pred[896]{0:T(1024)(128)(4,1)S(1)} %fusion.96), kind=kLoop, calls=%fused_computation.7.clone.1 | loop fusion | flops 8026368 | bytes 6437760 | tf_op jit(solution)/shard_map/while/body/eval_jaxpr/reduce_sum | solution.py:82
  92.2 5.8 %reduce-scatter.3.cloned.1.call-done = bf16[1,448,256]{2,1,0:T(8,128)(2,1)} async-done(((bf16[1,448,512]{2,1,0:T(8,128)(2,1)}), bf16[1,448,256]{2,1,0:T(8,128)(2,1)}) %reduce-scatter.3.cloned.1.call-update) | async-done | bytes 229392 | tf_op jit(solution)/shard_map/reduce_scatter | solution.py:105
  99.1 2.3 %all_gather.11 = bf16[1,448,512]{2,1,0:T(8,128)(2,1)S(1)} all-gather(bf16[1,448,256]{2,1,0:T(8,128)(2,1)S(1)} %fusion.37), channel_id=1, replica_groups=mesh['groups'=2,'tm'=4,'dp'=2,'head'=2] {'head'}, dimensions={2}, use_global_device_ids=true | all-gather | bytes 688128 | tf_op jit(solution)/shard_map/all_gather | solution.py:109
  101.9 3.6 %collective-permute-start = (bf16[1,15,256]{2,1,0:T(8,128)(2,1)S(1)}, bf16[1,15,256]{2,1,0:T(8,128)(2,1)S(1)}, u32[]{:S(2)}, u32[]{:S(2)}) collective-permute-start(bf16[1,15,256]{2,1,0:T(8,128)(2,1)S(1)} %get-tuple-element.198), channel_id=1, source_target_pairs={{0,4},{4,8},{8,12},{1,5},{5,9},{9,13},{2,6},{6,10},{10,14},{3,7},{... | collective-permute-start | bytes 23048 | tf_op jit(solution)/shard_map/ppermute | solution.py:15
  105.5 1.3 collective-permute-start.1
  107.8 3.3 %collective-permute-done.1 = bf16[1,15,256]{2,1,0:T(8,128)(2,1)S(1)} collective-permute-done((bf16[1,15,256]{2,1,0:T(8,128)(2,1)S(1)}, bf16[1,15,256]{2,1,0:T(8,128)(2,1)S(1)}, u32[]{:S(2)}, u32[]{:S(2)}) %collective-permute-start.1) | collective-permute-done | bytes 7712 | tf_op jit(solution)/shard_map/ppermute | solution.py:18
  111.1 4.0 %fusion.29 = bf16[1,448,512]{2,1,0:T(8,128)(2,1)} fusion(bf16[256,512]{1,0:T(8,128)(2,1)S(1)} %copy-done.12, bf16[1,448,256]{2,1,0:T(8,128)(2,1)S(1)} %fusion.39, bf16[1,15,256]{2,1,0:T(8,128)(2,1)S(1)} %collective-permute-done.1, bf16[1,15,256]{2,1,0:T(8,128)(2,1)S(1)} %collective-permute-done, f32[256]{0:T(256)S(1)} %bitcast.177, f32[256]{0:T(256)S(1)} %bitcast.178, ...), kind=kOutput, calls=%fused_computation.70 | convolution fusion | flops 139116544 | bytes 997376 | tf_op jit(solution)/shard_map/rsc,cd->rsd/dot_general | solution.py:121
  115.1 8.0 %reduce-scatter.5.cloned.1.call-done = bf16[1,448,256]{2,1,0:T(8,128)(2,1)} async-done(((bf16[1,448,512]{2,1,0:T(8,128)(2,1)}), bf16[1,448,256]{2,1,0:T(8,128)(2,1)}) %reduce-scatter.5.cloned.1.call-update) | async-done | bytes 229392 | tf_op jit(solution)/shard_map/reduce_scatter | solution.py:122
  124.1 1.6 %broadcast_in_dim.110 = f32[448,4,256]{2,1,0:T(4,128)} broadcast(f32[448,256]{1,0:T(8,128)S(1)} %add_bitcast_fusion), dimensions={0,2} | broadcast | bytes 2293760 | tf_op jit(solution)/shard_map/broadcast_in_dim | solution.py:126
  125.7 2.0 %broadcast_in_dim.111 = f32[1,1792,256]{2,1,0:T(8,128)S(1)} reshape(f32[448,4,256]{2,1,0:T(4,128)} %broadcast_in_dim.110) | data formatting | bytes 3670016 | tf_op jit(solution)/shard_map/broadcast_in_dim | solution.py:126
  127.7 1.3 fusion.27
  (75 shorter events, 11.1 us)
Async XLA Ops:
  6.5 94.8 %copy-start = (bf16[512,2,256]{2,1,0:T(2,128)(2,1)S(1)}, bf16[512,2,256]{2,1,0:T(2,128)(2,1)}, u32[]{:S(2)}) copy-start(bf16[512,2,256]{2,1,0:T(2,128)(2,1)} %param.20) | copy-start | bytes 1572868
  6.5 54.4 %all-gather.4.cloned.1.call-start = ((), (), s32[]{:S(2)}) async-start(), calls=%async_computation.4 | async-start | bytes 2293760 | tf_op jit(solution)/shard_map/all_gather | solution.py:52
  7.3 0.6 copy-start.8
  10.6 1.9 %copy-start.10 = (f32[4,256]{1,0:T(4,128)S(1)}, f32[4,256]{1,0:T(4,128)}, u32[]{:S(2)}) copy-start(f32[4,256]{1,0:T(4,128)} %param.15) | copy-start | bytes 12292
  12.5 4.5 %copy-start.5 = (bf16[512,128]{1,0:T(8,128)(2,1)S(1)}, bf16[512,128]{1,0:T(8,128)(2,1)}, u32[]{:S(2)}) copy-start(bf16[512,128]{1,0:T(8,128)(2,1)} %param.16) | copy-start | bytes 393220
  12.5 48.5 %copy-start.4 = (bf16[512,128]{1,0:T(8,128)(2,1)S(1)}, bf16[512,128]{1,0:T(8,128)(2,1)}, u32[]{:S(2)}) copy-start(bf16[512,128]{1,0:T(8,128)(2,1)} %param.17) | copy-start | bytes 393220
  13.8 0.7 copy-start.3
  16.9 46.5 %copy-start.7 = (bf16[512,48]{0,1:T(8,128)(2,1)S(1)}, bf16[512,48]{0,1:T(8,128)(2,1)}, u32[]{:S(2)}) copy-start(bf16[512,48]{0,1:T(8,128)(2,1)} %param.18) | copy-start | bytes 147460
  16.9 81.1 %reduce-scatter.3.cloned.1.call-start = ((), (), s32[]{:S(2)}) async-start(), calls=%async_computation.2 | async-start | bytes 688128 | tf_op jit(solution)/shard_map/reduce_scatter | solution.py:105
  61.0 2.4 %copy-start.1 = (bf16[1792,512]{1,0:T(8,128)(2,1)S(1)}, bf16[1792,512]{1,0:T(8,128)(2,1)}, u32[]{:S(2)}) copy-start(bf16[1792,512]{1,0:T(8,128)(2,1)} %all-gather.4.cloned.1.call-done) | copy-start | bytes 5505028
  64.1 25.9 %copy-start.6 = (bf16[48,512]{1,0:T(8,128)(2,1)S(1)}, bf16[48,512]{1,0:T(8,128)(2,1)}, u32[]{:S(2)}) copy-start(bf16[48,512]{1,0:T(8,128)(2,1)} %param.19) | copy-start | bytes 147460
  69.0 5.7 %slice-start = ((s8[6422528]{0:T(1024)(128)(4,1)}), s8[2228224]{0:T(1024)(128)(4,1)S(1)}, s32[]{:S(2)}) async-start(s8[6422528]{0:T(1024)(128)(4,1)} %bitcast.142), calls=%async_computation.5 | async-start | bytes 4456448 | tf_op jit(solution)/shard_map/while
  69.7 5.0 %slice-start.1 = ((s8[6422528]{0:T(1024)(128)(4,1)}), s8[4194304]{0:T(1024)(128)(4,1)S(1)}, s32[]{:S(2)}) async-start(s8[6422528]{0:T(1024)(128)(4,1)} %bitcast.142), calls=%async_computation.6 | async-start | bytes 8388608 | tf_op jit(solution)/shard_map/while
  81.5 5.7 %slice-start = ((s8[6422528]{0:T(1024)(128)(4,1)}), s8[2228224]{0:T(1024)(128)(4,1)S(1)}, s32[]{:S(2)}) async-start(s8[6422528]{0:T(1024)(128)(4,1)} %bitcast.142), calls=%async_computation.5 | async-start | bytes 4456448 | tf_op jit(solution)/shard_map/while
  82.1 5.0 %slice-start.1 = ((s8[6422528]{0:T(1024)(128)(4,1)}), s8[4194304]{0:T(1024)(128)(4,1)S(1)}, s32[]{:S(2)}) async-start(s8[6422528]{0:T(1024)(128)(4,1)} %bitcast.142), calls=%async_computation.6 | async-start | bytes 8388608 | tf_op jit(solution)/shard_map/while
  91.1 32.0 %reduce-scatter.5.cloned.1.call-start = ((), (), s32[]{:S(2)}) async-start(), calls=%async_computation.3 | async-start | bytes 688128 | tf_op jit(solution)/shard_map/reduce_scatter | solution.py:122
  99.1 12.0 %copy-start.12 = (bf16[256,512]{1,0:T(8,128)(2,1)S(1)}, bf16[256,512]{1,0:T(8,128)(2,1)}, u32[]{:S(2)}) copy-start(bf16[256,512]{1,0:T(8,128)(2,1)} %param.22) | copy-start | bytes 786436
  101.9 5.9 %collective-permute-start = (bf16[1,15,256]{2,1,0:T(8,128)(2,1)S(1)}, bf16[1,15,256]{2,1,0:T(8,128)(2,1)S(1)}, u32[]{:S(2)}, u32[]{:S(2)}) collective-permute-start(bf16[1,15,256]{2,1,0:T(8,128)(2,1)S(1)} %get-tuple-element.198), channel_id=1, source_target_pairs={{0,4},{4,8},{8,12},{1,5},{5,9},{9,13},{2,6},{6,10},{10,14},{3,7},{... | collective-permute-start | bytes 23048 | tf_op jit(solution)/shard_map/ppermute | solution.py:15
  105.5 5.5 %collective-permute-start.1 = (bf16[1,15,256]{2,1,0:T(8,128)(2,1)S(1)}, bf16[1,15,256]{2,1,0:T(8,128)(2,1)S(1)}, u32[]{:S(2)}, u32[]{:S(2)}) collective-permute-start(bf16[1,15,256]{2,1,0:T(8,128)(2,1)S(1)} %get-tuple-element.199), channel_id=1, source_target_pairs={{4,0},{8,4},{12,8},{5,1},{9,5},{13,9},{6,2},{10,6},{14,10},{7,3},{... | collective-permute-start | bytes 23048 | tf_op jit(solution)/shard_map/ppermute | solution.py:18
  125.6 2.0 %copy-start.2 = (bf16[1,1792,256]{2,1,0:T(8,128)(2,1)S(1)}, bf16[1,1792,256]{2,1,0:T(8,128)(2,1)}, u32[]{:S(2)}) copy-start(bf16[1,1792,256]{2,1,0:T(8,128)(2,1)} %param.13) | copy-start | bytes 2752516
  125.6 2.0 %copy-start.9 = (pred[1792]{0:T(1024)(128)(4,1)S(1)}, pred[1792]{0:T(1024)(128)(4,1)}, u32[]{:S(2)}) copy-start(pred[1792]{0:T(1024)(128)(4,1)} %copy-done.8) | copy-start | bytes 5380
  125.6 2.0 %copy-start.11 = (f32[256]{0:T(256)S(1)}, f32[256]{0:T(256)}, u32[]{:S(2)}) copy-start(f32[256]{0:T(256)} %param.23) | copy-start | bytes 3076
Sparse Core Ops, SparseCore 0:
  17.0 43.9 all-gather.3
  91.2 6.6 reduce-scatter.2
  115.2 7.8 reduce-scatter.4
where the time goes:
time: 136 us; the launch traced here: 135 us
  waiting for transfers between devices  59 us (43%)
  matrix products  29.4 us (22%)
  between operations  14.1 us (10%)
  other arithmetic  12.3 us (9%)
  local copies, waits for them, and re-layouts  11 us (8%)
  starting transfers between devices  4.96 us (4%)
  blocking collectives  4.64 us (3%)
    all_gather x1, waiting for transfers between devices, shards(): segment = lax.all_gather(full_rows, 'tm', axis=1, tiled=True)  41.9 us
    dot_general x2, matrix products, merge_block(): jnp.einsum('rhqk,rhvk->rhqv', expo.astype(jnp.bfloat16), value_rows, pref...  10.1 us
    dot_general x2, matrix products, merge_block(): jnp.einsum('rqhd,rhdk->rhqk', query_set, key_rows, preferred_element_type...  9.57 us
    reduce_scatter x1, waiting for transfers between devices, shards(): lax.psum_scatter(conv_part.astype(jnp.bfloat16), 'head', scatter_dimensio...  8.03 us
    reduce_scatter x1, waiting for transfers between devices, shards(): lax.psum_scatter(partial_value.astype(jnp.bfloat16), 'head', scatter_dime...  5.76 us
    dot_general x1, matrix products, shards(): jnp.einsum('rsc,cd->rsd', hidden, conv_out, preferred_element_type=jnp.fl...  3.97 us
    reduce_sum x2, other arithmetic, merge_block(): denominator = denominator * factor + jnp.sum(expo, axis=-1)  3.65 us
    ppermute x1, starting transfers between devices, with_halo(): lax.ppermute(lax.slice_in_dim(block, block.shape[dim] - width, None, axis...  3.59 us
  transfers between devices with their start and end apart: 5, of which 4 were waited for; matrix products, arithmetic and copies ran while one was open for 3% of the time, Pallas kernels for 0%

commit v1 on v0

--- a/solution.py
+++ b/solution.py
@@ -2,6 +2,7 @@
 import jax.numpy as jnp
 from jax import lax
 from jax.sharding import PartitionSpec as P
+from jax.lax import axis_index, axis_size, ppermute
 
 QDIM = 32
 VDIM = 12
@@ -49,7 +50,31 @@
     heads_here = w_query.shape[1] // QDIM
     queries = jnp.einsum("rsd,dk->rsk", full_rows, w_query, preferred_element_type=jnp.float32)
     queries = queries.astype(jnp.bfloat16).reshape(records, quarter, heads_here, QDIM)
-    segment = lax.all_gather(full_rows, "tm", axis=1, tiled=True)
+    t_next = axis_size("tm")
+    w1 = axis_index("tm")
+    built, r_now, latest = (t_next, w1, full_rows.shape[1])
+    parts_seen = []
+    for idx, c in enumerate(full_rows.shape):
+        parts_seen.append(c * built if idx == 1 else c)
+    raw_out = jnp.zeros(parts_seen, full_rows.dtype)
+    segment = lax.dynamic_update_slice_in_dim(raw_out, full_rows, r_now * latest, axis=1)
+    k_now = local_part = full_rows
+    for p in range(1, built // 2 + 1):
+        seen = []
+        for idx in range(built):
+            seen.append((idx, (idx + 1) % built))
+        k_now = ppermute(k_now, "tm", seen)
+        segment = lax.dynamic_update_slice_in_dim(
+            segment, k_now, (r_now - p) % built * latest, axis=1
+        )
+        if 2 * p < built:
+            row_list = []
+            for idx in range(built):
+                row_list.append((idx, (idx - 1) % built))
+            local_part = ppermute(local_part, "tm", perm=row_list)
+            segment = lax.dynamic_update_slice_in_dim(
+                segment, local_part, (r_now + p) % built * latest, axis=1
+            )
     keys_t = jnp.einsum("rnd,dk->rkn", segment, w_key, preferred_element_type=jnp.float32)
     values_t = jnp.einsum("rnd,dk->rkn", segment, w_value, preferred_element_type=jnp.float32)
     packed = jnp.concatenate([keys_t, values_t], axis=1).astype(jnp.bfloat16)

time: 136 us -> 126 us (0.926)
  waiting for transfers between devices: 59 us -> 46.5 us
  starting transfers between devices: 4.96 us -> 10.1 us
  matrix products: 29.4 us -> 26.7 us
    all_gather x1 -> x0, waiting for transfers between devices: 41.9 us -> none  [shards(): segment = lax.all_gather(full_rows, 'tm', axis=1, tiled=True)]
    ppermute x0 -> x3, waiting for transfers between devices: none -> 29.1 us  [the longest x2 20.4 us: shards(): k_now = ppermute(k_now, 'tm', seen)]
    ppermute x0 -> x3, starting transfers between devices: none -> 4.97 us  [the longest x2 2.94 us: shards(): k_now = ppermute(k_now, 'tm', seen)]
    dot_general x1, matrix products: 2.36 us -> 0.73 us  [shards(): jnp.einsum('rnd,dk->rkn', segment, w_key, preferred_element_type=jnp.floa...]
  transfers between devices with their start and end apart: 5 -> 7, of which waited for: 4 -> 6; matrix products, arithmetic and copies ran while one was open for 3% -> 3% of each run, Pallas kernels for 0% -> 0%
where the time goes in v1:
time: 126 us; the launch traced here: 125 us
  waiting for transfers between devices  46.5 us (37%)
  matrix products  26.7 us (21%)
  between operations  14.5 us (12%)
  other arithmetic  12.3 us (10%)
  local copies, waits for them, and re-layouts  10.5 us (8%)
  starting transfers between devices  10.1 us (8%)
  blocking collectives  4.52 us (4%)
    ppermute x2, waiting for transfers between devices, shards(): k_now = ppermute(k_now, 'tm', seen)  20.4 us
    dot_general x2, matrix products, merge_block(): jnp.einsum('rhqk,rhvk->rhqv', expo.astype(jnp.bfloat16), value_rows, pref...  10.1 us
    dot_general x2, matrix products, merge_block(): jnp.einsum('rqhd,rhdk->rhqk', query_set, key_rows, preferred_element_type...  9.58 us
    ppermute x1, waiting for transfers between devices, shards(): local_part = ppermute(local_part, 'tm', perm=row_list)  8.63 us
    reduce_scatter x1, waiting for transfers between devices, shards(): lax.psum_scatter(conv_part.astype(jnp.bfloat16), 'head', scatter_dimensio...  8.03 us
    reduce_scatter x1, waiting for transfers between devices, shards(): lax.psum_scatter(partial_value.astype(jnp.bfloat16), 'head', scatter_dime...  6.29 us
    dot_general x1, matrix products, shards(): jnp.einsum('rsc,cd->rsd', hidden, conv_out, preferred_element_type=jnp.fl...  3.97 us
    reduce_sum x2, other arithmetic, merge_block(): denominator = denominator * factor + jnp.sum(expo, axis=-1)  3.65 us
  transfers between devices with their start and end apart: 7, of which 6 were waited for; matrix products, arithmetic and copies ran while one was open for 3% of the time, Pallas kernels for 0%

profile of v1, /device:TPU:0, one launch (start us, length us, event | category | flops | bytes accessed | tf_op | source)
XLA Modules:
  0.0 125.3 jit_solution(5516409879806169344)
XLA Ops:
  7.8 2.7 %select_convert_fusion = f32[1,1792,256]{2,1,0:T(8,128)} fusion(bf16[1,1792,256]{2,1,0:T(8,128)(2,1)} %param.13, pred[1792]{0:T(1024)(128)(4,1)S(1)} %add_compare_fusion), kind=kLoop, calls=%fused_computation.72 | loop fusion | flops 917504 | bytes 2754304 | tf_op jit(solution)/shard_map/convert_element_type | solution.py:44
  10.6 1.8 %reshape.462 = f32[1,448,4,256]{3,2,1,0:T(4,128)S(1)} reshape(f32[1,1792,256]{2,1,0:T(8,128)} %select_convert_fusion) | data formatting | bytes 3670016 | tf_op jit(solution)/shard_map/convert_element_type | solution.py:44
  13.8 2.3 %all-gather = bf16[448,512]{1,0:T(8,128)(2,1)S(1)} all-gather(bf16[448,256]{1,0:T(8,128)(2,1)S(1)} %multiply_reduce_fusion), channel_id=2, replica_groups=mesh['groups'=2,'tm'=4,'dp'=2,'head'=2] {'head'}, dimensions={1}, use_global_device_ids=true | all-gather | bytes 688128 | tf_op jit(solution)/shard_map/all_gather | solution.py:49
  16.0 2.9 %collective-permute-start = (bf16[1,448,512]{2,1,0:T(8,128)(2,1)S(1)}, bf16[1,448,512]{2,1,0:T(8,128)(2,1)S(1)}, u32[]{:S(2)}, u32[]{:S(2)}) collective-permute-start(bf16[1,448,512]{2,1,0:T(8,128)(2,1)S(1)} %bitcast.152), channel_id=1, source_target_pairs={{0,4},{4,8},{8,12},{12,0},{1,5},{5,9},{9,13},{13,1},{2,6},{6,10},{... | collective-permute-start | bytes 1376264 | tf_op jit(solution)/shard_map/ppermute | solution.py:66
  19.0 2.0 %collective-permute-start.1 = (bf16[1,448,512]{2,1,0:T(8,128)(2,1)S(1)}, bf16[1,448,512]{2,1,0:T(8,128)(2,1)S(1)}, u32[]{:S(2)}, u32[]{:S(2)}) collective-permute-start(bf16[1,448,512]{2,1,0:T(8,128)(2,1)S(1)} %bitcast.153), channel_id=1, source_target_pairs={{0,12},{4,0},{8,4},{12,8},{1,13},{5,1},{9,5},{13,9},{2,14},{6,2},{... | collective-permute-start | bytes 1376264 | tf_op jit(solution)/shard_map/ppermute | solution.py:74
  22.4 10.1 %collective-permute-done = bf16[1,448,512]{2,1,0:T(8,128)(2,1)S(1)} collective-permute-done((bf16[1,448,512]{2,1,0:T(8,128)(2,1)S(1)}, bf16[1,448,512]{2,1,0:T(8,128)(2,1)S(1)}, u32[]{:S(2)}, u32[]{:S(2)}) %collective-permute-start) | collective-permute-done | bytes 458784 | tf_op jit(solution)/shard_map/ppermute | solution.py:66
  32.5 8.6 %collective-permute-done.1 = bf16[1,448,512]{2,1,0:T(8,128)(2,1)S(1)} collective-permute-done((bf16[1,448,512]{2,1,0:T(8,128)(2,1)S(1)}, bf16[1,448,512]{2,1,0:T(8,128)(2,1)S(1)}, u32[]{:S(2)}, u32[]{:S(2)}) %collective-permute-start.1) | collective-permute-done | bytes 458784 | tf_op jit(solution)/shard_map/ppermute | solution.py:74
  41.1 10.4 %collective-permute-done.2 = bf16[1,448,512]{2,1,0:T(8,128)(2,1)S(1)} collective-permute-done((bf16[1,448,512]{2,1,0:T(8,128)(2,1)S(1)}, bf16[1,448,512]{2,1,0:T(8,128)(2,1)S(1)}, u32[]{:S(2)}, u32[]{:S(2)}) %collective-permute-start.2) | collective-permute-done | bytes 458784 | tf_op jit(solution)/shard_map/ppermute | solution.py:66
  53.0 25.0 %while.18 = (s32[]{:T(128)}, f32[1,4,448]{2,1,0:T(4,128)S(1)}, f32[1,4,448]{2,1,0:T(4,128)S(1)}, f32[1,4,448,12]{2,3,1,0:T(8,128)}, s32[1]{0:T(128)}, /*index=5*...) while((s32[]{:T(128)}, f32[1,4,448]{2,1,0:T(4,128)S(1)}, ...), condition=%wide.region_4.5_spmd.clone, body=%wide.region_1.4_spmd.clone.sunk | while | flops 162245888 | bytes 40058620 | solution.py:122
  53.1 4.8 %bitcast_reduce_fusion.2 = (f32[4,448]{1,0:T(4,128)S(1)}, f32[4,896,448]{1,2,0:T(8,128)}) fusion(pred[896]{0:T(1024)(128)(4,1)S(1)} %fusion.96, bf16[4,32,896]{2,1,0:T(8,128)(2,1)S(1)} %bitcast.151, bf16[1,448,4,32]{1,3,2,0:T(8,128)(2,1)} %get-tuple-element.312), kind=kOutput, calls=%fused_computation.2.clone.1 | convolution fusion | flops 107575552 | bytes 6774656 | tf_op jit(solution)/shard_map/while/body/eval_jaxpr/rqhd,rhdk->rhqk/dot_general | solution.py:98
  58.6 5.0 %fusion.99 = f32[1,4,448,12]{2,3,1,0:T(8,128)} fusion(bf16[4,12,896]{2,1,0:T(8,128)(2,1)} %reshape.472, f32[4,896,448]{1,2,0:T(8,128)} %get-tuple-element.280, f32[4,448]{1,0:T(4,128)S(1)} %bitcast.154, pred[896]{0:T(1024)(128)(4,1)S(1)} %fusion.96, f32[1,4,448,12]{2,3,1,0:T(8,128)} %get-tuple-element.297, f32[4,448]{1,0:T(4,128)S(1)} %get-tuple-element.281, ...), kind=kOutput, calls=%fused_computation.12.clone.1 | convolution fusion | flops 46627840 | bytes 6695809 | tf_op jit(solution)/shard_map/while/body/eval_jaxpr/rhqk,rhvk->rhqv/dot_general | solution.py:108
  63.6 1.8 %fusion.98 = f32[4,448]{1,0:T(4,128)S(1)} fusion(f32[4,896,448]{1,2,0:T(8,128)S(1)} %bitcast.150, f32[4,448]{1,0:T(4,128)S(1)} %bitcast.155, pred[896]{0:T(1024)(128)(4,1)S(1)} %fusion.96), kind=kLoop, calls=%fused_computation.7.clone.1 | loop fusion | flops 8026368 | bytes 6437760 | tf_op jit(solution)/shard_map/while/body/eval_jaxpr/reduce_sum | solution.py:107
  65.6 4.8 %bitcast_reduce_fusion.2 = (f32[4,448]{1,0:T(4,128)S(1)}, f32[4,896,448]{1,2,0:T(8,128)}) fusion(pred[896]{0:T(1024)(128)(4,1)S(1)} %fusion.96, bf16[4,32,896]{2,1,0:T(8,128)(2,1)S(1)} %bitcast.151, bf16[1,448,4,32]{1,3,2,0:T(8,128)(2,1)} %get-tuple-element.312), kind=kOutput, calls=%fused_computation.2.clone.1 | convolution fusion | flops 107575552 | bytes 6774656 | tf_op jit(solution)/shard_map/while/body/eval_jaxpr/rqhd,rhdk->rhqk/dot_general | solution.py:98
  71.1 5.0 %fusion.99 = f32[1,4,448,12]{2,3,1,0:T(8,128)} fusion(bf16[4,12,896]{2,1,0:T(8,128)(2,1)} %reshape.472, f32[4,896,448]{1,2,0:T(8,128)} %get-tuple-element.280, f32[4,448]{1,0:T(4,128)S(1)} %bitcast.154, pred[896]{0:T(1024)(128)(4,1)S(1)} %fusion.96, f32[1,4,448,12]{2,3,1,0:T(8,128)} %get-tuple-element.297, f32[4,448]{1,0:T(4,128)S(1)} %get-tuple-element.281, ...), kind=kOutput, calls=%fused_computation.12.clone.1 | convolution fusion | flops 46627840 | bytes 6695809 | tf_op jit(solution)/shard_map/while/body/eval_jaxpr/rhqk,rhvk->rhqv/dot_general | solution.py:108
  76.1 1.8 %fusion.98 = f32[4,448]{1,0:T(4,128)S(1)} fusion(f32[4,896,448]{1,2,0:T(8,128)S(1)} %bitcast.150, f32[4,448]{1,0:T(4,128)S(1)} %bitcast.155, pred[896]{0:T(1024)(128)(4,1)S(1)} %fusion.96), kind=kLoop, calls=%fused_computation.7.clone.1 | loop fusion | flops 8026368 | bytes 6437760 | tf_op jit(solution)/shard_map/while/body/eval_jaxpr/reduce_sum | solution.py:107
  81.2 6.3 %reduce-scatter.3.cloned.1.call-done = bf16[1,448,256]{2,1,0:T(8,128)(2,1)} async-done(((bf16[1,448,512]{2,1,0:T(8,128)(2,1)}), bf16[1,448,256]{2,1,0:T(8,128)(2,1)}) %reduce-scatter.3.cloned.1.call-update) | async-done | bytes 229392 | tf_op jit(solution)/shard_map/reduce_scatter | solution.py:130
  88.6 2.3 %all_gather.7 = bf16[1,448,512]{2,1,0:T(8,128)(2,1)S(1)} all-gather(bf16[1,448,256]{2,1,0:T(8,128)(2,1)S(1)} %fusion.37), channel_id=1, replica_groups=mesh['groups'=2,'tm'=4,'dp'=2,'head'=2] {'head'}, dimensions={2}, use_global_device_ids=true | all-gather | bytes 688128 | tf_op jit(solution)/shard_map/all_gather | solution.py:134
  91.4 3.6 %collective-permute-start.3 = (bf16[1,15,256]{2,1,0:T(8,128)(2,1)S(1)}, bf16[1,15,256]{2,1,0:T(8,128)(2,1)S(1)}, u32[]{:S(2)}, u32[]{:S(2)}) collective-permute-start(bf16[1,15,256]{2,1,0:T(8,128)(2,1)S(1)} %get-tuple-element.198), channel_id=1, source_target_pairs={{0,4},{4,8},{8,12},{1,5},{5,9},{9,13},{2,6},{6,10},{10,14},{3,7},{... | collective-permute-start | bytes 23048 | tf_op jit(solution)/shard_map/ppermute | solution.py:16
  95.0 1.5 %collective-permute-start.4 = (bf16[1,15,256]{2,1,0:T(8,128)(2,1)S(1)}, bf16[1,15,256]{2,1,0:T(8,128)(2,1)S(1)}, u32[]{:S(2)}, u32[]{:S(2)}) collective-permute-start(bf16[1,15,256]{2,1,0:T(8,128)(2,1)S(1)} %get-tuple-element.199), channel_id=1, source_target_pairs={{4,0},{8,4},{12,8},{5,1},{9,5},{13,9},{6,2},{10,6},{14,10},{7,3},{... | collective-permute-start | bytes 23048 | tf_op jit(solution)/shard_map/ppermute | solution.py:19
  97.5 3.1 %collective-permute-done.4 = bf16[1,15,256]{2,1,0:T(8,128)(2,1)S(1)} collective-permute-done((bf16[1,15,256]{2,1,0:T(8,128)(2,1)S(1)}, bf16[1,15,256]{2,1,0:T(8,128)(2,1)S(1)}, u32[]{:S(2)}, u32[]{:S(2)}) %collective-permute-start.4) | collective-permute-done | bytes 7712 | tf_op jit(solution)/shard_map/ppermute | solution.py:19
  100.5 4.0 %fusion.29 = bf16[1,448,512]{2,1,0:T(8,128)(2,1)} fusion(bf16[256,512]{1,0:T(8,128)(2,1)S(1)} %copy-done.11, bf16[1,448,256]{2,1,0:T(8,128)(2,1)S(1)} %fusion.39, bf16[1,15,256]{2,1,0:T(8,128)(2,1)S(1)} %collective-permute-done.4, bf16[1,15,256]{2,1,0:T(8,128)(2,1)S(1)} %collective-permute-done.3, f32[256]{0:T(256)S(1)} %bitcast.186, f32[256]{0:T(256)S(1)} %bitcast.187, ...), kind=kOutput, calls=%fused_computation.70 | convolution fusion | flops 139116544 | bytes 997376 | tf_op jit(solution)/shard_map/rsc,cd->rsd/dot_general | solution.py:146
  104.5 8.0 %reduce-scatter.5.cloned.1.call-done = bf16[1,448,256]{2,1,0:T(8,128)(2,1)} async-done(((bf16[1,448,512]{2,1,0:T(8,128)(2,1)}), bf16[1,448,256]{2,1,0:T(8,128)(2,1)}) %reduce-scatter.5.cloned.1.call-update) | async-done | bytes 229392 | tf_op jit(solution)/shard_map/reduce_scatter | solution.py:147
  113.6 1.6 %broadcast_in_dim.111 = f32[448,4,256]{2,1,0:T(4,128)} broadcast(f32[448,256]{1,0:T(8,128)S(1)} %add_bitcast_fusion), dimensions={0,2} | broadcast | bytes 2293760 | tf_op jit(solution)/shard_map/broadcast_in_dim | solution.py:151
  115.1 2.0 %broadcast_in_dim.112 = f32[1,1792,256]{2,1,0:T(8,128)S(1)} reshape(f32[448,4,256]{2,1,0:T(4,128)} %broadcast_in_dim.111) | data formatting | bytes 3670016 | tf_op jit(solution)/shard_map/broadcast_in_dim | solution.py:151
  (81 shorter events, 14.2 us)
Async XLA Ops:
  6.5 84.3 %copy-start = (bf16[512,2,256]{2,1,0:T(2,128)(2,1)S(1)}, bf16[512,2,256]{2,1,0:T(2,128)(2,1)}, u32[]{:S(2)}) copy-start(bf16[512,2,256]{2,1,0:T(2,128)(2,1)} %param.20) | copy-start | bytes 1572868
  6.5 80.9 %reduce-scatter.3.cloned.1.call-start = ((), (), s32[]{:S(2)}) async-start(), calls=%async_computation.2 | async-start | bytes 688128 | tf_op jit(solution)/shard_map/reduce_scatter | solution.py:130
  7.3 0.6 copy-start.7
  10.6 1.9 %copy-start.9 = (f32[4,256]{1,0:T(4,128)S(1)}, f32[4,256]{1,0:T(4,128)}, u32[]{:S(2)}) copy-start(f32[4,256]{1,0:T(4,128)} %param.15) | copy-start | bytes 12292
  12.5 8.6 %copy-start.4 = (bf16[512,128]{1,0:T(8,128)(2,1)S(1)}, bf16[512,128]{1,0:T(8,128)(2,1)}, u32[]{:S(2)}) copy-start(bf16[512,128]{1,0:T(8,128)(2,1)} %param.16) | copy-start | bytes 393220
  13.8 2.3 %copy-start.2 = (bf16[448,256]{1,0:T(8,128)(2,1)}, bf16[448,256]{1,0:T(8,128)(2,1)S(1)}, u32[]{:S(2)}) copy-start(bf16[448,256]{1,0:T(8,128)(2,1)S(1)} %multiply_reduce_fusion) | copy-start | bytes 688132
  16.0 16.4 %collective-permute-start = (bf16[1,448,512]{2,1,0:T(8,128)(2,1)S(1)}, bf16[1,448,512]{2,1,0:T(8,128)(2,1)S(1)}, u32[]{:S(2)}, u32[]{:S(2)}) collective-permute-start(bf16[1,448,512]{2,1,0:T(8,128)(2,1)S(1)} %bitcast.152), channel_id=1, source_target_pairs={{0,4},{4,8},{8,12},{12,0},{1,5},{5,9},{9,13},{13,1},{2,6},{6,10},{... | collective-permute-start | bytes 1376264 | tf_op jit(solution)/shard_map/ppermute | solution.py:66
  19.0 22.1 %collective-permute-start.1 = (bf16[1,448,512]{2,1,0:T(8,128)(2,1)S(1)}, bf16[1,448,512]{2,1,0:T(8,128)(2,1)S(1)}, u32[]{:S(2)}, u32[]{:S(2)}) collective-permute-start(bf16[1,448,512]{2,1,0:T(8,128)(2,1)S(1)} %bitcast.153), channel_id=1, source_target_pairs={{0,12},{4,0},{8,4},{12,8},{1,13},{5,1},{9,5},{13,9},{2,14},{6,2},{... | collective-permute-start | bytes 1376264 | tf_op jit(solution)/shard_map/ppermute | solution.py:74
  22.3 29.3 %copy-start.3 = (bf16[512,128]{1,0:T(8,128)(2,1)S(1)}, bf16[512,128]{1,0:T(8,128)(2,1)}, u32[]{:S(2)}) copy-start(bf16[512,128]{1,0:T(8,128)(2,1)} %param.17) | copy-start | bytes 393220
  32.4 19.1 %collective-permute-start.2 = (bf16[1,448,512]{2,1,0:T(8,128)(2,1)S(1)}, bf16[1,448,512]{2,1,0:T(8,128)(2,1)S(1)}, u32[]{:S(2)}, u32[]{:S(2)}) collective-permute-start(bf16[1,448,512]{2,1,0:T(8,128)(2,1)S(1)} %collective-permute-done), channel_id=1, source_target_pairs={{0,4},{4,8},{8,12},{12,0},{1,5},{5,9},{9,13},{13,1},{2,6},{6,10},{... | collective-permute-start | bytes 1376264 | tf_op jit(solution)/shard_map/ppermute | solution.py:66
  41.1 11.2 %copy-start.6 = (bf16[512,48]{0,1:T(8,128)(2,1)S(1)}, bf16[512,48]{0,1:T(8,128)(2,1)}, u32[]{:S(2)}) copy-start(bf16[512,48]{0,1:T(8,128)(2,1)} %param.18) | copy-start | bytes 147460
  53.0 25.9 %copy-start.5 = (bf16[48,512]{1,0:T(8,128)(2,1)S(1)}, bf16[48,512]{1,0:T(8,128)(2,1)}, u32[]{:S(2)}) copy-start(bf16[48,512]{1,0:T(8,128)(2,1)} %param.19) | copy-start | bytes 147460
  57.9 5.7 %slice-start = ((s8[6422528]{0:T(1024)(128)(4,1)}), s8[2228224]{0:T(1024)(128)(4,1)S(1)}, s32[]{:S(2)}) async-start(s8[6422528]{0:T(1024)(128)(4,1)} %bitcast.149), calls=%async_computation.4 | async-start | bytes 4456448 | tf_op jit(solution)/shard_map/while
  58.6 5.0 %slice-start.1 = ((s8[6422528]{0:T(1024)(128)(4,1)}), s8[4194304]{0:T(1024)(128)(4,1)S(1)}, s32[]{:S(2)}) async-start(s8[6422528]{0:T(1024)(128)(4,1)} %bitcast.149), calls=%async_computation.5 | async-start | bytes 8388608 | tf_op jit(solution)/shard_map/while
  70.4 5.7 %slice-start = ((s8[6422528]{0:T(1024)(128)(4,1)}), s8[2228224]{0:T(1024)(128)(4,1)S(1)}, s32[]{:S(2)}) async-start(s8[6422528]{0:T(1024)(128)(4,1)} %bitcast.149), calls=%async_computation.4 | async-start | bytes 4456448 | tf_op jit(solution)/shard_map/while
  71.1 5.0 %slice-start.1 = ((s8[6422528]{0:T(1024)(128)(4,1)}), s8[4194304]{0:T(1024)(128)(4,1)S(1)}, s32[]{:S(2)}) async-start(s8[6422528]{0:T(1024)(128)(4,1)} %bitcast.149), calls=%async_computation.5 | async-start | bytes 8388608 | tf_op jit(solution)/shard_map/while
  80.1 32.5 %reduce-scatter.5.cloned.1.call-start = ((), (), s32[]{:S(2)}) async-start(), calls=%async_computation.3 | async-start | bytes 688128 | tf_op jit(solution)/shard_map/reduce_scatter | solution.py:147
  88.5 12.0 %copy-start.11 = (bf16[256,512]{1,0:T(8,128)(2,1)S(1)}, bf16[256,512]{1,0:T(8,128)(2,1)}, u32[]{:S(2)}) copy-start(bf16[256,512]{1,0:T(8,128)(2,1)} %param.22) | copy-start | bytes 786436
  91.4 6.1 %collective-permute-start.3 = (bf16[1,15,256]{2,1,0:T(8,128)(2,1)S(1)}, bf16[1,15,256]{2,1,0:T(8,128)(2,1)S(1)}, u32[]{:S(2)}, u32[]{:S(2)}) collective-permute-start(bf16[1,15,256]{2,1,0:T(8,128)(2,1)S(1)} %get-tuple-element.198), channel_id=1, source_target_pairs={{0,4},{4,8},{8,12},{1,5},{5,9},{9,13},{2,6},{6,10},{10,14},{3,7},{... | collective-permute-start | bytes 23048 | tf_op jit(solution)/shard_map/ppermute | solution.py:16
  95.0 5.5 %collective-permute-start.4 = (bf16[1,15,256]{2,1,0:T(8,128)(2,1)S(1)}, bf16[1,15,256]{2,1,0:T(8,128)(2,1)S(1)}, u32[]{:S(2)}, u32[]{:S(2)}) collective-permute-start(bf16[1,15,256]{2,1,0:T(8,128)(2,1)S(1)} %get-tuple-element.199), channel_id=1, source_target_pairs={{4,0},{8,4},{12,8},{5,1},{9,5},{13,9},{6,2},{10,6},{14,10},{7,3},{... | collective-permute-start | bytes 23048 | tf_op jit(solution)/shard_map/ppermute | solution.py:19
  115.1 2.0 %copy-start.1 = (bf16[1,1792,256]{2,1,0:T(8,128)(2,1)S(1)}, bf16[1,1792,256]{2,1,0:T(8,128)(2,1)}, u32[]{:S(2)}) copy-start(bf16[1,1792,256]{2,1,0:T(8,128)(2,1)} %param.13) | copy-start | bytes 2752516
  115.1 2.0 %copy-start.8 = (pred[1792]{0:T(1024)(128)(4,1)S(1)}, pred[1792]{0:T(1024)(128)(4,1)}, u32[]{:S(2)}) copy-start(pred[1792]{0:T(1024)(128)(4,1)} %copy-done.7) | copy-start | bytes 5380
  115.1 2.0 %copy-start.10 = (f32[256]{0:T(256)S(1)}, f32[256]{0:T(256)}, u32[]{:S(2)}) copy-start(f32[256]{0:T(256)} %param.23) | copy-start | bytes 3076
Sparse Core Ops, SparseCore 0:
  80.2 7.2 reduce-scatter.2
  104.7 7.8 reduce-scatter.4
